TPU v7x, 32 devices: a whole 2x2x4 slice. The times are simulated.
32 devices in a mesh: rows: 8 (over y, x, core), cols: 4 (over z).
Axes of the slice: x: 2, y: 2, z: 4, core: 2. Of those that a mesh axis runs over, the one named last changes fastest.
Arguments:
- irradiance_layers: bfloat16 [2, 2048, 16384], P(None, ('rows', 'cols')), may hold values from 0 to 2
- initial_heat_anomaly: float32 [2, 2048, 16384], P(None, 'rows', 'cols'), may hold values from -12 to 12
- drift_rate_eastward: float32 [2, 2048, 16384], P(None, 'rows', 'cols'), may hold values from 0.35 to 0.45
- drift_rate_northward: float32 [2, 2048, 16384], P(None, 'rows', 'cols'), may hold values from 0.33 to 0.4
- extinction_factor: float32 [2, 2048, 16384], P(None, 'rows', 'cols'), may hold values from 0.1 to 1
- windward_polarity_eastward: int32 [2, 2048], P(None, 'rows'), may hold values from 0 to 1
- windward_polarity_northward: int32 [2, 16384], P(None, 'cols'), may hold values from 0 to 1
Outputs:
- phase_slabs: float32 [2, 2048, 16384], P(None, ('rows', 'cols'))
- temperature_end: float32 [2, 2048, 16384], P(None, 'rows', 'cols')
Inputs may be any that keep to these rules, and one draw needn't show every extreme that they name: `windward_polarity_eastward`: 1 means wind plus slew toward increasing x. `windward_polarity_northward`: 1 means wind plus slew toward increasing y.
All inputs are finite; a program needn't handle non-finite values.
Results may differ from a plain program's by a relative error of at most 0.0003.
Values may be sent and summed in bfloat16 or wider, within the bound.
No kernel may reach another device: no remote copies, remote signals or barrier semaphores. Data moves between devices by JAX's collectives and lax.ppermute only.
A program may use at most 192 MiB of HBM per device.

v0:
```python
import jax
import jax.numpy as jnp
from jax import lax
from jax.sharding import PartitionSpec as P

SUBSTEPS = 4
DIFFUSION = 0.03
HEAT_RATE = 0.25


def extended(block, sides, width):
    for axis, dim in sides:
        count = lax.axis_size(axis)
        forward = [(i, i + 1) for i in range(count - 1)]
        backward = [(target, source) for source, target in forward]
        low = lax.ppermute(
            lax.slice_in_dim(block, block.shape[dim] - width, None, axis=dim), axis, forward
        )
        high = lax.ppermute(lax.slice_in_dim(block, 0, width, axis=dim), axis, backward)
        block = jnp.concatenate([low, block, high], axis=dim)
    return block


def advance(padded, wind_x, wind_y, heating):
    middle = padded[1:-1, 1:-1]
    west_cell = padded[1:-1, :-2]
    east_cell = padded[1:-1, 2:]
    south_cell = padded[:-2, 1:-1]
    north_cell = padded[2:, 1:-1]
    upwind_x = jnp.where(wind_x > 0, west_cell, east_cell)
    upwind_y = jnp.where(wind_y > 0, south_cell, north_cell)
    neighbours = west_cell + east_cell + south_cell + north_cell - 4.0 * middle
    return (
        middle
        - jnp.abs(wind_x) * (middle - upwind_x)
        - jnp.abs(wind_y) * (middle - upwind_y)
        + DIFFUSION * neighbours
        + heating
    )


def body(
    irradiance_layers,
    initial_heat_anomaly,
    drift_rate_eastward,
    drift_rate_northward,
    extinction_factor,
    windward_polarity_eastward,
    windward_polarity_northward,
):
    optical_layers = initial_heat_anomaly.shape[0]
    arrived = lax.all_to_all(irradiance_layers, "cols", split_axis=2, concat_axis=1, tiled=True)
    phases = []
    finals = []
    for optical_layer in range(optical_layers):
        light_tile = arrived[optical_layer]
        wind_x = jnp.where(
            windward_polarity_eastward[optical_layer][:, None] == 1,
            drift_rate_eastward[optical_layer],
            -drift_rate_eastward[optical_layer],
        )
        wind_y = jnp.where(
            windward_polarity_northward[optical_layer][None, :] == 1,
            drift_rate_northward[optical_layer],
            -drift_rate_northward[optical_layer],
        )
        heating = HEAT_RATE * extinction_factor[optical_layer] * light_tile.astype(jnp.float32)
        heat_transport_advance = initial_heat_anomaly[optical_layer]
        phase_sum = jnp.zeros_like(heat_transport_advance)
        for section_index in range(SUBSTEPS):
            padded = extended(heat_transport_advance, (("rows", 0), ("cols", 1)), 1)
            heat_transport_advance = advance(padded, wind_x, wind_y, heating)
            phase_sum = phase_sum + heat_transport_advance / SUBSTEPS
        phases.append(phase_sum)
        finals.append(heat_transport_advance)
    phase_slabs = lax.all_to_all(jnp.stack(phases), "cols", split_axis=1, concat_axis=2, tiled=True)
    return (phase_slabs, jnp.stack(finals))


def solution(mesh):
    return jax.shard_map(
        body,
        mesh=mesh,
        in_specs=(
            P(None, ("rows", "cols"), None),
            P(None, "rows", "cols"),
            P(None, "rows", "cols"),
            P(None, "rows", "cols"),
            P(None, "rows", "cols"),
            P(None, "rows"),
            P(None, "cols"),
        ),
        out_specs=(P(None, ("rows", "cols"), None), P(None, "rows", "cols")),
        check_vma=False,
    )
```

profile of v0, /device:TPU:3, one launch (start us, length us, event | category | flops | bytes accessed | tf_op | source)
XLA Modules:
  0.0 627.5 jit_solution(5142534280835631980)
XLA Ops:
  0.6 17.8 %copy.19 = bf16[2,64,16384]{1,0,2:T(2,128)(2,1)} copy(bf16[2,64,16384]{2,1,0:T(8,128)(2,1)} %param.7) | data formatting | bytes 8388608 | tf_op args[0]
  18.4 9.6 %reshape.44 = bf16[4,2,262144]{2,1,0:T(2,128)(2,1)} reshape(bf16[16384,2,64]{2,1,0:T(2,128)(2,1)} %bitcast.140) | data formatting | bytes 8388608
  28.0 5.0 all-to-all-start
  61.0 64.7 %all-to-all-done = bf16[4,2,262144]{2,1,0:T(2,128)(2,1)} async-done(((bf16[4,2,262144]{2,1,0:T(2,128)(2,1)}), bf16[4,2,262144]{2,1,0:T(2,128)(2,1)}, u32[]{:S(2)}, u32[]{:S(2)}) %all-to-all-start) | async-done | bytes 4194336 | tf_op jit(solution)/shard_map/all_to_all | solution.py:52
  125.6 9.3 %reshape.45 = bf16[16384,2,64]{2,1,0:T(2,128)(2,1)} reshape(bf16[4,2,262144]{2,1,0:T(2,128)(2,1)} %all-to-all-done) | data formatting | bytes 8388608
  134.9 18.6 %copy.21 = bf16[2,64,4,4096]{3,1,2,0:T(8,128)(2,1)} copy(bf16[2,64,4,4096]{1,0,3,2:T(2,128)(2,1)} %bitcast.139) | data formatting | bytes 8388608 | tf_op jit(solution)/shard_map/all_to_all | solution.py:52
  158.4 20.0 %add_add_fusion.7 = (f32[256,4096]{1,0:T(8,128)S(1)}, pred[256,4096]{1,0:T(8,128)(4,1)}, pred[256,4096]{1,0:T(8,128)(4,1)}) fusion(f32[256,4096]{1,0:T(8,128)} %copy-done.8, f32[1,4096]{1,0:T(1,128)S(1)} %collective-permute-done, f32[1,4096]{1,0:T(1,128)S(1)} %collective-permute-done.1, f32[258,1]{1,0:T(8,128)} %copy-done.12, f32[258,1]{1,0:T(8,128)} %copy-done.13, ...), kind=kLoop, calls=%fused_computation.82 | loop fusion | flops 36700160 | bytes 25205008 | tf_op jit(solution)/shard_map/add | solution.py:34
  178.5 5.6 collective-permute-start.4
  186.2 19.6 %add_add_fusion.3 = (f32[256,4096]{1,0:T(8,128)S(1)}, pred[256,4096]{1,0:T(8,128)(4,1)}, pred[256,4096]{1,0:T(8,128)(4,1)}) fusion(f32[256,4096]{1,0:T(8,128)} %copy-done.7, f32[1,4096]{1,0:T(1,128)S(1)} %collective-permute-done.16, f32[1,4096]{1,0:T(1,128)S(1)} %collective-permute-done.17, f32[258,1]{1,0:T(8,128)S(1)} %collective-permute-done.18, ...), kind=kLoop, calls=%fused_computation.76 | loop fusion | flops 36700160 | bytes 25205008 | tf_op jit(solution)/shard_map/add | solution.py:34
  221.9 12.6 %add_add_fusion.6 = f32[256,4096]{1,0:T(8,128)} fusion(f32[256,4096]{1,0:T(8,128)S(1)} %get-tuple-element.8, pred[256,4096]{1,0:T(8,128)(4,1)} %get-tuple-element.10, f32[1,4096]{1,0:T(1,128)S(1)} %collective-permute-done.4, f32[1,4096]{1,0:T(1,128)S(1)} %collective-permute-done.5, pred[256,4096]{1,0:T(8,128)(4,1)} %get-tuple-element.9, ...), kind=kLoop, calls=%fused_computation.81 | loop fusion | flops 34603008 | bytes 25205008 | tf_op jit(solution)/shard_map/add | solution.py:34
  236.2 5.1 collective-permute-start.8
  243.2 18.1 %add_add_fusion.2 = f32[256,4096]{1,0:T(8,128)} fusion(f32[256,4096]{1,0:T(8,128)} %copy-done, pred[256,4096]{1,0:T(8,128)(4,1)} %get-tuple-element.15, f32[1,4096]{1,0:T(1,128)S(1)} %collective-permute-done.20, f32[1,4096]{1,0:T(1,128)} %copy-done.22, pred[256,4096]{1,0:T(8,128)(4,1)} %get-tuple-element.14, f32[258,1]{1,0:T(8,128)S(1)} %collective-permute-done.22, ...), kind=kLoop, calls=%fused_computation.75 | loop fusion | flops 34603008 | bytes 25205008 | tf_op jit(solution)/shard_map/add | solution.py:34
  282.5 18.8 %add_add_fusion.5 = f32[256,4096]{1,0:T(8,128)} fusion(f32[256,4096]{1,0:T(8,128)} %add_add_fusion.6, pred[256,4096]{1,0:T(8,128)(4,1)} %get-tuple-element.10, f32[1,4096]{1,0:T(1,128)S(1)} %collective-permute-done.8, f32[1,4096]{1,0:T(1,128)S(1)} %collective-permute-done.9, pred[256,4096]{1,0:T(8,128)(4,1)} %get-tuple-element.9, f32[258,1]{1,0:T(8,128)} %copy-done.15, ...), kind=kLoop, calls=%fused_computation.80 | loop fusion | flops 34603008 | bytes 25205008 | tf_op jit(solution)/shard_map/add | solution.py:34
  302.9 5.4 collective-permute-start.12
  310.2 18.1 %add_add_fusion.1 = f32[256,4096]{1,0:T(8,128)} fusion(f32[256,4096]{1,0:T(8,128)} %add_add_fusion.2, pred[256,4096]{1,0:T(8,128)(4,1)} %get-tuple-element.15, f32[1,4096]{1,0:T(1,128)S(1)} %collective-permute-done.24, f32[1,4096]{1,0:T(1,128)} %copy-done.23, pred[256,4096]{1,0:T(8,128)(4,1)} %get-tuple-element.14, f32[258,1]{1,0:T(8,128)S(1)} %collective-permute-done.26, ...), kind=kLoop, calls=%fused_computation.74 | loop fusion | flops 34603008 | bytes 25205008 | tf_op jit(solution)/shard_map/add | solution.py:34
  351.4 20.9 %multiply_bitcast_fusion = (f32[1,256,4096]{2,1,0:T(8,128)}, f32[256,4096]{1,0:T(8,128)}) fusion(f32[256,4096]{1,0:T(8,128)} %add_add_fusion.5, f32[256,4096]{1,0:T(8,128)S(1)} %get-tuple-element.8, f32[256,4096]{1,0:T(8,128)S(1)} %copy-done.2, bf16[1,4,64,4096]{3,2,1,0:T(8,128)(2,1)S(1)} %copy-done.6, f32[2,256,4096]{2,1,0:T(8,128)} %param.11, ...), kind=kLoop, calls=%fused_computation.78 | loop fusion | flops 38797312 | bytes 37787920 | tf_op jit(solution)/shard_map/stack | solution.py:76
  372.3 8.7 %copy.22 = f32[1,256,4096]{2,0,1:T(1,128)} copy(f32[1,256,4096]{2,1,0:T(8,128)} %get-tuple-element.6) | data formatting | bytes 8388608 | tf_op jit(solution)/shard_map/stack | solution.py:76
  381.1 19.5 %add_multiply_fusion = (f32[256,4096]{1,0:T(8,128)S(1)}, f32[256,4096]{1,0:T(8,128)}) fusion(f32[256,4096]{1,0:T(8,128)} %add_add_fusion.1, f32[256,4096]{1,0:T(8,128)S(1)} %copy-done.1, f32[256,4096]{1,0:T(8,128)} %add_add_fusion.2, bf16[1,4,64,4096]{3,2,1,0:T(8,128)(2,1)S(1)} %copy-done.4, f32[2,256,4096]{2,1,0:T(8,128)} %param.11, ...), kind=kLoop, calls=%fused_computation.72 | loop fusion | flops 38797312 | bytes 37787920 | tf_op jit(solution)/shard_map/add | solution.py:73
  405.2 9.2 %pad_maximum_fusion = f32[2,256,4096]{2,0,1:T(2,128)} fusion(f32[1,256,4096]{2,0,1:T(1,128)S(1)} %stack.19, f32[1,256,4096]{2,0,1:T(1,128)S(1)} %copy-done.11), kind=kLoop, calls=%fused_computation | loop fusion | flops 2097152 | bytes 16777216 | tf_op jit(solution)/shard_map/stack | solution.py:76
  414.4 6.8 %all-to-all-start.1 = ((f32[2,256,4096]{2,0,1:T(2,128)}), f32[2,256,4096]{2,0,1:T(2,128)}, u32[]{:S(2)}, u32[]{:S(2)}) async-start(f32[2,256,4096]{2,0,1:T(2,128)} %pad_maximum_fusion), calls=%async_computation.1 | async-start | bytes 16777216 | tf_op jit(solution)/shard_map/all_to_all | solution.py:76
  421.2 7.9 %pad_maximum_fusion.1 = f32[2,256,4096]{2,1,0:T(8,128)} fusion(f32[1,256,4096]{2,1,0:T(8,128)} %bitcast.143, f32[1,256,4096]{2,1,0:T(8,128)} %bitcast.142), kind=kLoop, calls=%fused_computation.1 | loop fusion | flops 2097152 | bytes 16777216 | tf_op jit(solution)/shard_map/stack | solution.py:77
  429.0 175.3 %all-to-all-done.1 = f32[2,256,4096]{2,0,1:T(2,128)} async-done(((f32[2,256,4096]{2,0,1:T(2,128)}), f32[2,256,4096]{2,0,1:T(2,128)}, u32[]{:S(2)}, u32[]{:S(2)}) %all-to-all-start.1) | async-done | bytes 8388640 | tf_op jit(solution)/shard_map/all_to_all | solution.py:76
  604.3 12.1 %copy.23 = f32[2,64,4,4096]{3,2,1,0:T(4,128)} copy(f32[2,64,4,4096]{3,0,1,2:T(2,128)} %bitcast.18) | data formatting | bytes 16777216 | tf_op jit(solution)/shard_map/all_to_all | solution.py:76
  616.4 10.9 %all_to_all.30 = f32[2,64,16384]{2,1,0:T(8,128)} reshape(f32[2,64,4,4096]{3,2,1,0:T(4,128)} %copy.23) | data formatting | bytes 16777216 | tf_op jit(solution)/shard_map/all_to_all | solution.py:76
  (152 shorter events, 106.4 us)
Async XLA Ops:
  28.0 97.7 %all-to-all-start = ((bf16[4,2,262144]{2,1,0:T(2,128)(2,1)}), bf16[4,2,262144]{2,1,0:T(2,128)(2,1)}, u32[]{:S(2)}, u32[]{:S(2)}) async-start(bf16[4,2,262144]{2,1,0:T(2,128)(2,1)} %reshape.44), calls=%async_computation | async-start | bytes 8388608 | tf_op jit(solution)/shard_map/all_to_all | solution.py:52
  34.1 16.3 %collective-permute-start = (f32[1,4096]{1,0:T(1,128)S(1)}, f32[1,4096]{1,0:T(1,128)S(1)}, u32[]{:S(2)}, u32[]{:S(2)}) collective-permute-start(f32[1,4096]{1,0:T(1,128)S(1)} %get-tuple-element.17), channel_id=1, source_target_pairs={{0,4},{4,8},{8,12},{12,16},{16,20},{20,24},{24,28},{1,5},{5,9},{9,... | collective-permute-start | bytes 49160 | tf_op jit(solution)/shard_map/ppermute | solution.py:16
  37.8 12.6 %collective-permute-start.1 = (f32[1,4096]{1,0:T(1,128)S(1)}, f32[1,4096]{1,0:T(1,128)S(1)}, u32[]{:S(2)}, u32[]{:S(2)}) collective-permute-start(f32[1,4096]{1,0:T(1,128)S(1)} %get-tuple-element.16), channel_id=1, source_target_pairs={{4,0},{8,4},{12,8},{16,12},{20,16},{24,20},{28,24},{5,1},{9,5},{13... | collective-permute-start | bytes 49160 | tf_op jit(solution)/shard_map/ppermute | solution.py:19
  39.7 15.8 %collective-permute-start.16 = (f32[1,4096]{1,0:T(1,128)S(1)}, f32[1,4096]{1,0:T(1,128)S(1)}, u32[]{:S(2)}, u32[]{:S(2)}) collective-permute-start(f32[1,4096]{1,0:T(1,128)S(1)} %get-tuple-element.19), channel_id=1, source_target_pairs={{0,4},{4,8},{8,12},{12,16},{16,20},{20,24},{24,28},{1,5},{5,9},{9,... | collective-permute-start | bytes 49160 | tf_op jit(solution)/shard_map/ppermute | solution.py:16
  50.5 107.2 %collective-permute-start.2 = (f32[258,1]{1,0:T(8,128)S(1)}, f32[258,1]{1,0:T(8,128)S(1)}, u32[]{:S(2)}, u32[]{:S(2)}) collective-permute-start(f32[258,1]{1,0:T(8,128)S(1)} %get-tuple-element.29), channel_id=1, source_target_pairs={{0,1},{1,2},{2,3},{4,5},{5,6},{6,7},{8,9},{9,10},{10,11},{12,13},{... | collective-permute-start | bytes 3104 | tf_op jit(solution)/shard_map/ppermute | solution.py:16
  54.2 103.5 %collective-permute-start.3 = (f32[258,1]{1,0:T(8,128)S(1)}, f32[258,1]{1,0:T(8,128)S(1)}, u32[]{:S(2)}, u32[]{:S(2)}) collective-permute-start(f32[258,1]{1,0:T(8,128)S(1)} %get-tuple-element.28), channel_id=1, source_target_pairs={{1,0},{2,1},{3,2},{5,4},{6,5},{7,6},{9,8},{10,9},{11,10},{13,12},{... | collective-permute-start | bytes 3104 | tf_op jit(solution)/shard_map/ppermute | solution.py:19
  55.7 130.4 %collective-permute-start.18 = (f32[258,1]{1,0:T(8,128)S(1)}, f32[258,1]{1,0:T(8,128)S(1)}, u32[]{:S(2)}, u32[]{:S(2)}) collective-permute-start(f32[258,1]{1,0:T(8,128)S(1)} %get-tuple-element.37), channel_id=1, source_target_pairs={{0,1},{1,2},{2,3},{4,5},{5,6},{6,7},{8,9},{9,10},{10,11},{12,13},{... | collective-permute-start | bytes 3104 | tf_op jit(solution)/shard_map/ppermute | solution.py:16
  59.7 126.4 %collective-permute-start.19 = (f32[258,1]{1,0:T(8,128)S(1)}, f32[258,1]{1,0:T(8,128)}, u32[]{:S(2)}, u32[]{:S(2)}) collective-permute-start(f32[258,1]{1,0:T(8,128)S(1)} %get-tuple-element.36), channel_id=1, source_target_pairs={{1,0},{2,1},{3,2},{5,4},{6,5},{7,6},{9,8},{10,9},{11,10},{13,12},{... | collective-permute-start | bytes 3104 | tf_op jit(solution)/shard_map/ppermute | solution.py:19
  178.5 33.7 %collective-permute-start.4 = (f32[1,4096]{1,0:T(1,128)S(1)}, f32[1,4096]{1,0:T(1,128)S(1)}, u32[]{:S(2)}, u32[]{:S(2)}) collective-permute-start(f32[1,4096]{1,0:T(1,128)S(1)} %get-tuple-element.43), channel_id=1, source_target_pairs={{0,4},{4,8},{8,12},{12,16},{16,20},{20,24},{24,28},{1,5},{5,9},{9,... | collective-permute-start | bytes 49160 | tf_op jit(solution)/shard_map/ppermute | solution.py:16
  184.1 28.1 %collective-permute-start.5 = (f32[1,4096]{1,0:T(1,128)S(1)}, f32[1,4096]{1,0:T(1,128)S(1)}, u32[]{:S(2)}, u32[]{:S(2)}) collective-permute-start(f32[1,4096]{1,0:T(1,128)S(1)} %get-tuple-element.42), channel_id=1, source_target_pairs={{4,0},{8,4},{12,8},{16,12},{20,16},{24,20},{28,24},{5,1},{9,5},{13... | collective-permute-start | bytes 49160 | tf_op jit(solution)/shard_map/ppermute | solution.py:19
  216.4 26.8 %collective-permute-start.22 = (f32[258,1]{1,0:T(8,128)S(1)}, f32[258,1]{1,0:T(8,128)S(1)}, u32[]{:S(2)}, u32[]{:S(2)}) collective-permute-start(f32[258,1]{1,0:T(8,128)S(1)} %get-tuple-element.35), channel_id=1, source_target_pairs={{0,1},{1,2},{2,3},{4,5},{5,6},{6,7},{8,9},{9,10},{10,11},{12,13},{... | collective-permute-start | bytes 3104 | tf_op jit(solution)/shard_map/ppermute | solution.py:16
  219.3 23.9 %collective-permute-start.23 = (f32[258,1]{1,0:T(8,128)S(1)}, f32[258,1]{1,0:T(8,128)}, u32[]{:S(2)}, u32[]{:S(2)}) collective-permute-start(f32[258,1]{1,0:T(8,128)S(1)} %get-tuple-element.34), channel_id=1, source_target_pairs={{1,0},{2,1},{3,2},{5,4},{6,5},{7,6},{9,8},{10,9},{11,10},{13,12},{... | collective-permute-start | bytes 3104 | tf_op jit(solution)/shard_map/ppermute | solution.py:19
  236.2 32.9 %collective-permute-start.8 = (f32[1,4096]{1,0:T(1,128)}, f32[1,4096]{1,0:T(1,128)S(1)}, u32[]{:S(2)}, u32[]{:S(2)}) collective-permute-start(f32[1,4096]{1,0:T(1,128)} %get-tuple-element.41), channel_id=1, source_target_pairs={{0,4},{4,8},{8,12},{12,16},{16,20},{20,24},{24,28},{1,5},{5,9},{9,... | collective-permute-start | bytes 49160 | tf_op jit(solution)/shard_map/ppermute | solution.py:16
  241.3 27.8 %collective-permute-start.9 = (f32[1,4096]{1,0:T(1,128)}, f32[1,4096]{1,0:T(1,128)S(1)}, u32[]{:S(2)}, u32[]{:S(2)}) collective-permute-start(f32[1,4096]{1,0:T(1,128)} %get-tuple-element.40), channel_id=1, source_target_pairs={{4,0},{8,4},{12,8},{16,12},{20,16},{24,20},{28,24},{5,1},{9,5},{13... | collective-permute-start | bytes 49160 | tf_op jit(solution)/shard_map/ppermute | solution.py:19
  262.4 13.3 %collective-permute-start.24 = (f32[1,4096]{1,0:T(1,128)S(1)}, f32[1,4096]{1,0:T(1,128)S(1)}, u32[]{:S(2)}, u32[]{:S(2)}) collective-permute-start(f32[1,4096]{1,0:T(1,128)S(1)} %get-tuple-element.49), channel_id=1, source_target_pairs={{0,4},{4,8},{8,12},{12,16},{16,20},{20,24},{24,28},{1,5},{5,9},{9,... | collective-permute-start | bytes 49160 | tf_op jit(solution)/shard_map/ppermute | solution.py:16
  276.3 33.9 %collective-permute-start.26 = (f32[258,1]{1,0:T(8,128)S(1)}, f32[258,1]{1,0:T(8,128)S(1)}, u32[]{:S(2)}, u32[]{:S(2)}) collective-permute-start(f32[258,1]{1,0:T(8,128)S(1)} %get-tuple-element.33), channel_id=1, source_target_pairs={{0,1},{1,2},{2,3},{4,5},{5,6},{6,7},{8,9},{9,10},{10,11},{12,13},{... | collective-permute-start | bytes 3104 | tf_op jit(solution)/shard_map/ppermute | solution.py:16
  280.3 29.9 %collective-permute-start.27 = (f32[258,1]{1,0:T(8,128)S(1)}, f32[258,1]{1,0:T(8,128)}, u32[]{:S(2)}, u32[]{:S(2)}) collective-permute-start(f32[258,1]{1,0:T(8,128)S(1)} %get-tuple-element.32), channel_id=1, source_target_pairs={{1,0},{2,1},{3,2},{5,4},{6,5},{7,6},{9,8},{10,9},{11,10},{13,12},{... | collective-permute-start | bytes 3104 | tf_op jit(solution)/shard_map/ppermute | solution.py:19
  302.9 33.3 %collective-permute-start.12 = (f32[1,4096]{1,0:T(1,128)}, f32[1,4096]{1,0:T(1,128)S(1)}, u32[]{:S(2)}, u32[]{:S(2)}) collective-permute-start(f32[1,4096]{1,0:T(1,128)} %get-tuple-element.38), channel_id=1, source_target_pairs={{0,4},{4,8},{8,12},{12,16},{16,20},{20,24},{24,28},{1,5},{5,9},{9,... | collective-permute-start | bytes 49160 | tf_op jit(solution)/shard_map/ppermute | solution.py:16
  308.3 28.0 %collective-permute-start.13 = (f32[1,4096]{1,0:T(1,128)S(1)}, f32[1,4096]{1,0:T(1,128)S(1)}, u32[]{:S(2)}, u32[]{:S(2)}) collective-permute-start(f32[1,4096]{1,0:T(1,128)S(1)} %get-tuple-element.39), channel_id=1, source_target_pairs={{4,0},{8,4},{12,8},{16,12},{20,16},{24,20},{28,24},{5,1},{9,5},{13... | collective-permute-start | bytes 49160 | tf_op jit(solution)/shard_map/ppermute | solution.py:19
  329.3 13.7 %collective-permute-start.28 = (f32[1,4096]{1,0:T(1,128)S(1)}, f32[1,4096]{1,0:T(1,128)S(1)}, u32[]{:S(2)}, u32[]{:S(2)}) collective-permute-start(f32[1,4096]{1,0:T(1,128)S(1)} %get-tuple-element.46), channel_id=1, source_target_pairs={{0,4},{4,8},{8,12},{12,16},{16,20},{20,24},{24,28},{1,5},{5,9},{9,... | collective-permute-start | bytes 49160 | tf_op jit(solution)/shard_map/ppermute | solution.py:16
  337.4 13.9 %collective-permute-start.14 = (f32[258,1]{1,0:T(8,128)S(1)}, f32[258,1]{1,0:T(8,128)S(1)}, u32[]{:S(2)}, u32[]{:S(2)}) collective-permute-start(f32[258,1]{1,0:T(8,128)S(1)} %get-tuple-element.22), channel_id=1, source_target_pairs={{0,1},{1,2},{2,3},{4,5},{5,6},{6,7},{8,9},{9,10},{10,11},{12,13},{... | collective-permute-start | bytes 3104 | tf_op jit(solution)/shard_map/ppermute | solution.py:16
  344.8 36.2 %collective-permute-start.30 = (f32[258,1]{1,0:T(8,128)}, f32[258,1]{1,0:T(8,128)S(1)}, u32[]{:S(2)}, u32[]{:S(2)}) collective-permute-start(f32[258,1]{1,0:T(8,128)} %get-tuple-element.30), channel_id=1, source_target_pairs={{0,1},{1,2},{2,3},{4,5},{5,6},{6,7},{8,9},{9,10},{10,11},{12,13},{... | collective-permute-start | bytes 3104 | tf_op jit(solution)/shard_map/ppermute | solution.py:16
  349.6 31.4 %collective-permute-start.31 = (f32[258,1]{1,0:T(8,128)S(1)}, f32[258,1]{1,0:T(8,128)S(1)}, u32[]{:S(2)}, u32[]{:S(2)}) collective-permute-start(f32[258,1]{1,0:T(8,128)S(1)} %get-tuple-element.31), channel_id=1, source_target_pairs={{1,0},{2,1},{3,2},{5,4},{6,5},{7,6},{9,8},{10,9},{11,10},{13,12},{... | collective-permute-start | bytes 3104 | tf_op jit(solution)/shard_map/ppermute | solution.py:19
  414.4 189.9 %all-to-all-start.1 = ((f32[2,256,4096]{2,0,1:T(2,128)}), f32[2,256,4096]{2,0,1:T(2,128)}, u32[]{:S(2)}, u32[]{:S(2)}) async-start(f32[2,256,4096]{2,0,1:T(2,128)} %pad_maximum_fusion), calls=%async_computation.1 | async-start | bytes 16777216 | tf_op jit(solution)/shard_map/all_to_all | solution.py:76
  (44 other events, 794.5 us)
where the time goes:
time: 638 us; the launch traced here: 628 us
  waiting for transfers between devices  242 us (38%)
  other arithmetic  169 us (26%)
  local copies, waits for them, and re-layouts  109 us (17%)
  starting transfers between devices  106 us (17%)
    all_to_all x1, waiting for transfers between devices, body(): lax.all_to_all(jnp.stack(phases), 'cols', split_axis=1, concat_axis=2, ti...  175 us
    add x6, other arithmetic, advance(): middle - jnp.abs(wind_x) * (middle - upwind_x)  107 us
    ppermute x16, starting transfers between devices, extended(): lax.ppermute(lax.slice_in_dim(block, block.shape[dim] - width, None, axis...  67.2 us
    all_to_all x1, waiting for transfers between devices, body(): lax.all_to_all(irradiance_layers, 'cols', split_axis=2, concat_axis=1, ti...  64.7 us
    unnamed x71, local copies, waits for them, and re-layouts  39.5 us
    another operation x2, other arithmetic, body(): jnp.stack(phases)  30.1 us
    ppermute x16, starting transfers between devices, extended(): lax.ppermute(lax.slice_in_dim(block, 0, width, axis=dim), axis, backward)  26.7 us
    all_to_all x2, local copies, waits for them, and re-layouts, body(): lax.all_to_all(jnp.stack(phases), 'cols', split_axis=1, concat_axis=2, ti...  23 us
  transfers between devices with their start and end apart: 34, of which 4 were waited for; matrix products, arithmetic and copies ran while one was open for 31% of the time, Pallas kernels for 0%

commit v1 on v0

--- a/solution.py
+++ b/solution.py
@@ -6,6 +6,17 @@
 SUBSTEPS = 4
 DIFFUSION = 0.03
 HEAT_RATE = 0.25
+
+
+def in_blocks(array, dim, size):
+    before, after = (array.shape[:dim], array.shape[dim + 1 :])
+    return jnp.moveaxis(array.reshape(*before, size, -1, *after), dim, 0)
+
+
+def laid_out(blocks, dim):
+    shape = list(blocks.shape[1:])
+    shape[dim] *= blocks.shape[0]
+    return jnp.moveaxis(blocks, 0, dim).reshape(shape)
 
 
 def extended(block, sides, width):
@@ -73,7 +84,15 @@
             phase_sum = phase_sum + heat_transport_advance / SUBSTEPS
         phases.append(phase_sum)
         finals.append(heat_transport_advance)
-    phase_slabs = lax.all_to_all(jnp.stack(phases), "cols", split_axis=1, concat_axis=2, tiled=True)
+    x = jnp.stack(phases)
+    peers, mine = (lax.axis_size("cols"), lax.axis_index("cols"))
+    parts = in_blocks(x, 1, peers)
+    finished = [parts[mine]]
+    for step in range(1, peers):
+        sent = parts[mine ^ step]
+        finished.append(lax.ppermute(sent, "cols", [(i_2, i_2 ^ step) for i_2 in range(peers)]))
+    parts = jnp.stack(finished)[mine ^ jnp.arange(peers)]
+    phase_slabs = laid_out(parts, 2)
     return (phase_slabs, jnp.stack(finals))
 
 

time: 638 us -> 612 us (0.959)
  the two profiles are of different devices: /device:TPU:3 before, /device:TPU:19 now
where the time goes in v1:
time: 612 us; the launch traced here: 601 us
  waiting for transfers between devices  232 us (38%)
  other arithmetic  166 us (27%)
  starting transfers between devices  109 us (18%)
  local copies, waits for them, and re-layouts  92.2 us (15%)
    ppermute x3, waiting for transfers between devices, body(): lax.ppermute(sent, 'cols', [(i_2, i_2 ^ step) for i_2 in range(peers)])  176 us
    add x6, other arithmetic, advance(): middle - jnp.abs(wind_x) * (middle - upwind_x)  107 us
    ppermute x16, starting transfers between devices, extended(): lax.ppermute(lax.slice_in_dim(block, block.shape[dim] - width, None, axis...  69 us
    all_to_all x1, waiting for transfers between devices, body(): lax.all_to_all(irradiance_layers, 'cols', split_axis=2, concat_axis=1, ti...  55.9 us
    add x2, other arithmetic, body(): phase_sum = phase_sum + heat_transport_advance / SUBSTEPS  42.2 us
    unnamed x59, local copies, waits for them, and re-layouts  39.3 us
    ppermute x16, starting transfers between devices, extended(): lax.ppermute(lax.slice_in_dim(block, 0, width, axis=dim), axis, backward)  32.2 us
    all_to_all x1, local copies, waits for them, and re-layouts, body(): lax.all_to_all(irradiance_layers, 'cols', split_axis=2, concat_axis=1, ti...  18.6 us
  transfers between devices with their start and end apart: 36, of which 4 were waited for; matrix products, arithmetic and copies ran while one was open for 31% of the time, Pallas kernels for 0%

profile of v1, /device:TPU:19, one launch (start us, length us, event | category | flops | bytes accessed | tf_op | source)
XLA Modules:
  0.0 601.3 jit_solution(9972487017976849196)
XLA Ops:
  0.6 17.8 %copy.27 = bf16[2,64,16384]{1,0,2:T(2,128)(2,1)} copy(bf16[2,64,16384]{2,1,0:T(8,128)(2,1)} %param.7) | data formatting | bytes 8388608 | tf_op args[0]
  18.4 9.6 %reshape.84 = bf16[4,2,262144]{2,1,0:T(2,128)(2,1)} reshape(bf16[16384,2,64]{2,1,0:T(2,128)(2,1)} %bitcast.160) | data formatting | bytes 8388608
  28.0 5.0 all-to-all-start
  46.7 7.8 %slice_bitcast_fusion = (f32[256,4096]{1,0:T(8,128)}, f32[256,4096]{1,0:T(8,128)}) fusion(f32[2,256,4096]{2,1,0:T(8,128)} %param.8), kind=kLoop, calls=%fused_computation.86 | loop fusion | bytes 16777216 | tf_op jit(solution)/shard_map/squeeze | solution.py:79
  66.7 55.9 %all-to-all-done = bf16[4,2,262144]{2,1,0:T(2,128)(2,1)} async-done(((bf16[4,2,262144]{2,1,0:T(2,128)(2,1)}), bf16[4,2,262144]{2,1,0:T(2,128)(2,1)}, u32[]{:S(2)}, u32[]{:S(2)}) %all-to-all-start) | async-done | bytes 4194336 | tf_op jit(solution)/shard_map/all_to_all | solution.py:63
  122.6 9.3 %reshape.85 = bf16[16384,2,64]{2,1,0:T(2,128)(2,1)} reshape(bf16[4,2,262144]{2,1,0:T(2,128)(2,1)} %all-to-all-done) | data formatting | bytes 8388608
  131.8 18.6 %copy.29 = bf16[2,64,4,4096]{3,1,2,0:T(8,128)(2,1)} copy(bf16[2,64,4,4096]{1,0,3,2:T(2,128)(2,1)} %bitcast.159) | data formatting | bytes 8388608 | tf_op jit(solution)/shard_map/all_to_all | solution.py:63
  155.3 20.9 %add_add_fusion.3 = (f32[256,4096]{1,0:T(8,128)S(1)}, pred[256,4096]{1,0:T(8,128)(4,1)}, pred[256,4096]{1,0:T(8,128)(4,1)}) fusion(f32[256,4096]{1,0:T(8,128)} %get-tuple-element.24, f32[1,4096]{1,0:T(1,128)S(1)} %collective-permute-done.16, f32[1,4096]{1,0:T(1,128)S(1)} %collective-permute-done.17, f32[258,1]{1,0:T(8,128)} %copy-done.11, ...), kind=kLoop, calls=%fused_computation.85 | loop fusion | flops 36700160 | bytes 25205008 | tf_op jit(solution)/shard_map/add | solution.py:45
  176.2 5.7 collective-permute-start.20
  183.9 18.8 %add_add_fusion.7 = (f32[256,4096]{1,0:T(8,128)S(1)}, pred[256,4096]{1,0:T(8,128)(4,1)}, pred[256,4096]{1,0:T(8,128)(4,1)}) fusion(f32[256,4096]{1,0:T(8,128)} %get-tuple-element.25, f32[1,4096]{1,0:T(1,128)S(1)} %collective-permute-done, f32[1,4096]{1,0:T(1,128)S(1)} %collective-permute-done.1, f32[258,1]{1,0:T(8,128)S(1)} %collective-permute-done.2, ...), kind=kLoop, calls=%fused_computation.91 | loop fusion | flops 36700160 | bytes 25205008 | tf_op jit(solution)/shard_map/add | solution.py:45
  222.7 12.5 %add_add_fusion.2 = f32[256,4096]{1,0:T(8,128)} fusion(f32[256,4096]{1,0:T(8,128)S(1)} %get-tuple-element.8, pred[256,4096]{1,0:T(8,128)(4,1)} %get-tuple-element.10, f32[1,4096]{1,0:T(1,128)S(1)} %collective-permute-done.20, f32[1,4096]{1,0:T(1,128)S(1)} %collective-permute-done.21, pred[256,4096]{1,0:T(8,128)(4,1)} %get-tuple-element.9, ...), kind=kLoop, calls=%fused_computation.84 | loop fusion | flops 34603008 | bytes 25205008 | tf_op jit(solution)/shard_map/add | solution.py:45
  236.8 5.4 collective-permute-start.24
  244.1 18.0 %add_add_fusion.6 = f32[256,4096]{1,0:T(8,128)} fusion(f32[256,4096]{1,0:T(8,128)} %copy-done, pred[256,4096]{1,0:T(8,128)(4,1)} %get-tuple-element.15, f32[1,4096]{1,0:T(1,128)S(1)} %collective-permute-done.4, f32[1,4096]{1,0:T(1,128)} %copy-done.16, pred[256,4096]{1,0:T(8,128)(4,1)} %get-tuple-element.14, f32[258,1]{1,0:T(8,128)S(1)} %collective-permute-done.6, ...), kind=kLoop, calls=%fused_computation.90 | loop fusion | flops 34603008 | bytes 25205008 | tf_op jit(solution)/shard_map/add | solution.py:45
  284.2 18.9 %add_add_fusion.1 = f32[256,4096]{1,0:T(8,128)} fusion(f32[256,4096]{1,0:T(8,128)} %add_add_fusion.2, pred[256,4096]{1,0:T(8,128)(4,1)} %get-tuple-element.10, f32[1,4096]{1,0:T(1,128)S(1)} %collective-permute-done.24, f32[1,4096]{1,0:T(1,128)S(1)} %collective-permute-done.25, pred[256,4096]{1,0:T(8,128)(4,1)} %get-tuple-element.9, f32[258,1]{1,0:T(8,128)} %copy-done.14, ...), kind=kLoop, calls=%fused_computation.83 | loop fusion | flops 34603008 | bytes 25205008 | tf_op jit(solution)/shard_map/add | solution.py:45
  304.8 5.4 collective-permute-start.28
  312.1 18.1 %add_add_fusion.5 = f32[256,4096]{1,0:T(8,128)} fusion(f32[256,4096]{1,0:T(8,128)} %add_add_fusion.6, pred[256,4096]{1,0:T(8,128)(4,1)} %get-tuple-element.15, f32[1,4096]{1,0:T(1,128)S(1)} %collective-permute-done.8, f32[1,4096]{1,0:T(1,128)} %copy-done.17, pred[256,4096]{1,0:T(8,128)(4,1)} %get-tuple-element.14, f32[258,1]{1,0:T(8,128)S(1)} %collective-permute-done.10, ...), kind=kLoop, calls=%fused_computation.89 | loop fusion | flops 34603008 | bytes 25205008 | tf_op jit(solution)/shard_map/add | solution.py:45
  352.2 21.0 %add_multiply_fusion = (f32[256,4096]{1,0:T(8,128)}, f32[256,4096]{1,0:T(8,128)}) fusion(f32[256,4096]{1,0:T(8,128)} %add_add_fusion.1, f32[256,4096]{1,0:T(8,128)S(1)} %get-tuple-element.8, f32[256,4096]{1,0:T(8,128)} %add_add_fusion.2, bf16[1,4,64,4096]{3,2,1,0:T(8,128)(2,1)} %copy-done.4, f32[2,256,4096]{2,1,0:T(8,128)} %param.11, ...), kind=kLoop, calls=%fused_computation.81 | loop fusion | flops 38797312 | bytes 37787920 | tf_op jit(solution)/shard_map/add | solution.py:84
  373.3 21.2 %add_multiply_fusion.1 = (f32[256,4096]{1,0:T(8,128)}, f32[256,4096]{1,0:T(8,128)}) fusion(f32[256,4096]{1,0:T(8,128)} %add_add_fusion.5, f32[256,4096]{1,0:T(8,128)S(1)} %copy-done.1, f32[256,4096]{1,0:T(8,128)} %add_add_fusion.6, bf16[1,4,64,4096]{3,2,1,0:T(8,128)(2,1)S(1)} %copy-done.3, f32[2,256,4096]{2,1,0:T(8,128)S(1)} %bitcast.155, ...), kind=kLoop, calls=%fused_computation.87 | loop fusion | flops 38797312 | bytes 37787920 | tf_op jit(solution)/shard_map/add | solution.py:84
  404.2 81.9 %collective-permute-done.32 = f32[2,64,4096]{2,1,0:T(8,128)S(1)} collective-permute-done((f32[2,64,4096]{2,1,0:T(8,128)S(1)}, f32[2,64,4096]{2,1,0:T(8,128)S(1)}, u32[]{:S(2)}, u32[]{:S(2)}) %collective-permute-start.32) | collective-permute-done | bytes 2097184 | tf_op jit(solution)/shard_map/ppermute | solution.py:93
  486.0 47.9 %collective-permute-done.33 = f32[2,64,4096]{2,1,0:T(8,128)S(1)} collective-permute-done((f32[2,64,4096]{2,1,0:T(8,128)S(1)}, f32[2,64,4096]{2,1,0:T(8,128)S(1)}, u32[]{:S(2)}, u32[]{:S(2)}) %collective-permute-start.33) | collective-permute-done | bytes 2097184 | tf_op jit(solution)/shard_map/ppermute | solution.py:93
  533.9 46.6 %collective-permute-done.34 = f32[2,64,4096]{2,1,0:T(8,128)} collective-permute-done((f32[2,64,4096]{2,1,0:T(8,128)S(1)}, f32[2,64,4096]{2,1,0:T(8,128)}, u32[]{:S(2)}, u32[]{:S(2)}) %collective-permute-start.34) | collective-permute-done | bytes 2097184 | tf_op jit(solution)/shard_map/ppermute | solution.py:93
  580.5 4.9 pad_maximum_fusion
  585.4 7.8 %gather_fusion = f32[4,2,64,4096]{3,2,1,0:T(8,128)} fusion(f32[4,2,64,4096]{3,2,1,0:T(8,128)} %pad_maximum_fusion, s32[1024]{0:T(1024)S(1)} %pad_clamp_fusion), kind=kCustom, calls=%fused_computation | custom fusion | bytes 16777232 | tf_op jit(solution)/shard_map/gather | solution.py:94
  593.3 7.8 %copy.35 = f32[4,2,8,8,4096]{4,3,0,2,1:T(8,128)} copy(f32[4,2,8,8,4096]{4,3,2,1,0:T(8,128)} %bitcast.158) | data formatting | bytes 16777216 | tf_op jit(solution)/shard_map/reshape | solution.py:19
  (146 shorter events, 112.7 us)
Async XLA Ops:
  28.0 94.6 %all-to-all-start = ((bf16[4,2,262144]{2,1,0:T(2,128)(2,1)}), bf16[4,2,262144]{2,1,0:T(2,128)(2,1)}, u32[]{:S(2)}, u32[]{:S(2)}) async-start(bf16[4,2,262144]{2,1,0:T(2,128)(2,1)} %reshape.84), calls=%async_computation | async-start | bytes 8388608 | tf_op jit(solution)/shard_map/all_to_all | solution.py:63
  34.2 20.4 %collective-permute-start.16 = (f32[1,4096]{1,0:T(1,128)S(1)}, f32[1,4096]{1,0:T(1,128)S(1)}, u32[]{:S(2)}, u32[]{:S(2)}) collective-permute-start(f32[1,4096]{1,0:T(1,128)S(1)} %get-tuple-element.23), channel_id=1, source_target_pairs={{0,4},{4,8},{8,12},{12,16},{16,20},{20,24},{24,28},{1,5},{5,9},{9,... | collective-permute-start | bytes 49160 | tf_op jit(solution)/shard_map/ppermute | solution.py:27
  38.1 16.5 %collective-permute-start.17 = (f32[1,4096]{1,0:T(1,128)S(1)}, f32[1,4096]{1,0:T(1,128)S(1)}, u32[]{:S(2)}, u32[]{:S(2)}) collective-permute-start(f32[1,4096]{1,0:T(1,128)S(1)} %get-tuple-element.20), channel_id=1, source_target_pairs={{4,0},{8,4},{12,8},{16,12},{20,16},{24,20},{28,24},{5,1},{9,5},{13... | collective-permute-start | bytes 49160 | tf_op jit(solution)/shard_map/ppermute | solution.py:30
  40.0 21.2 %collective-permute-start = (f32[1,4096]{1,0:T(1,128)S(1)}, f32[1,4096]{1,0:T(1,128)S(1)}, u32[]{:S(2)}, u32[]{:S(2)}) collective-permute-start(f32[1,4096]{1,0:T(1,128)S(1)} %get-tuple-element.22), channel_id=1, source_target_pairs={{0,4},{4,8},{8,12},{12,16},{16,20},{20,24},{24,28},{1,5},{5,9},{9,... | collective-permute-start | bytes 49160 | tf_op jit(solution)/shard_map/ppermute | solution.py:27
  44.6 16.7 %collective-permute-start.1 = (f32[1,4096]{1,0:T(1,128)S(1)}, f32[1,4096]{1,0:T(1,128)S(1)}, u32[]{:S(2)}, u32[]{:S(2)}) collective-permute-start(f32[1,4096]{1,0:T(1,128)S(1)} %get-tuple-element.21), channel_id=1, source_target_pairs={{4,0},{8,4},{12,8},{16,12},{20,16},{24,20},{28,24},{5,1},{9,5},{13... | collective-permute-start | bytes 49160 | tf_op jit(solution)/shard_map/ppermute | solution.py:30
  55.8 98.7 %collective-permute-start.18 = (f32[258,1]{1,0:T(8,128)S(1)}, f32[258,1]{1,0:T(8,128)S(1)}, u32[]{:S(2)}, u32[]{:S(2)}) collective-permute-start(f32[258,1]{1,0:T(8,128)S(1)} %get-tuple-element.33), channel_id=1, source_target_pairs={{0,1},{1,2},{2,3},{4,5},{5,6},{6,7},{8,9},{9,10},{10,11},{12,13},{... | collective-permute-start | bytes 3104 | tf_op jit(solution)/shard_map/ppermute | solution.py:27
  59.0 95.5 %collective-permute-start.19 = (f32[258,1]{1,0:T(8,128)S(1)}, f32[258,1]{1,0:T(8,128)S(1)}, u32[]{:S(2)}, u32[]{:S(2)}) collective-permute-start(f32[258,1]{1,0:T(8,128)S(1)} %get-tuple-element.32), channel_id=1, source_target_pairs={{1,0},{2,1},{3,2},{5,4},{6,5},{7,6},{9,8},{10,9},{11,10},{13,12},{... | collective-permute-start | bytes 3104 | tf_op jit(solution)/shard_map/ppermute | solution.py:30
  61.4 122.4 %collective-permute-start.2 = (f32[258,1]{1,0:T(8,128)S(1)}, f32[258,1]{1,0:T(8,128)S(1)}, u32[]{:S(2)}, u32[]{:S(2)}) collective-permute-start(f32[258,1]{1,0:T(8,128)S(1)} %get-tuple-element.41), channel_id=1, source_target_pairs={{0,1},{1,2},{2,3},{4,5},{5,6},{6,7},{8,9},{9,10},{10,11},{12,13},{... | collective-permute-start | bytes 3104 | tf_op jit(solution)/shard_map/ppermute | solution.py:27
  64.5 119.3 %collective-permute-start.3 = (f32[258,1]{1,0:T(8,128)S(1)}, f32[258,1]{1,0:T(8,128)}, u32[]{:S(2)}, u32[]{:S(2)}) collective-permute-start(f32[258,1]{1,0:T(8,128)S(1)} %get-tuple-element.40), channel_id=1, source_target_pairs={{1,0},{2,1},{3,2},{5,4},{6,5},{7,6},{9,8},{10,9},{11,10},{13,12},{... | collective-permute-start | bytes 3104 | tf_op jit(solution)/shard_map/ppermute | solution.py:30
  176.2 33.0 %collective-permute-start.20 = (f32[1,4096]{1,0:T(1,128)S(1)}, f32[1,4096]{1,0:T(1,128)S(1)}, u32[]{:S(2)}, u32[]{:S(2)}) collective-permute-start(f32[1,4096]{1,0:T(1,128)S(1)} %get-tuple-element.47), channel_id=1, source_target_pairs={{0,4},{4,8},{8,12},{12,16},{16,20},{20,24},{24,28},{1,5},{5,9},{9,... | collective-permute-start | bytes 49160 | tf_op jit(solution)/shard_map/ppermute | solution.py:27
  181.9 27.4 %collective-permute-start.21 = (f32[1,4096]{1,0:T(1,128)S(1)}, f32[1,4096]{1,0:T(1,128)S(1)}, u32[]{:S(2)}, u32[]{:S(2)}) collective-permute-start(f32[1,4096]{1,0:T(1,128)S(1)} %get-tuple-element.46), channel_id=1, source_target_pairs={{4,0},{8,4},{12,8},{16,12},{20,16},{24,20},{28,24},{5,1},{9,5},{13... | collective-permute-start | bytes 49160 | tf_op jit(solution)/shard_map/ppermute | solution.py:30
  215.6 28.5 %collective-permute-start.6 = (f32[258,1]{1,0:T(8,128)S(1)}, f32[258,1]{1,0:T(8,128)S(1)}, u32[]{:S(2)}, u32[]{:S(2)}) collective-permute-start(f32[258,1]{1,0:T(8,128)S(1)} %get-tuple-element.39), channel_id=1, source_target_pairs={{0,1},{1,2},{2,3},{4,5},{5,6},{6,7},{8,9},{9,10},{10,11},{12,13},{... | collective-permute-start | bytes 3104 | tf_op jit(solution)/shard_map/ppermute | solution.py:27
  219.5 24.7 %collective-permute-start.7 = (f32[258,1]{1,0:T(8,128)S(1)}, f32[258,1]{1,0:T(8,128)}, u32[]{:S(2)}, u32[]{:S(2)}) collective-permute-start(f32[258,1]{1,0:T(8,128)S(1)} %get-tuple-element.38), channel_id=1, source_target_pairs={{1,0},{2,1},{3,2},{5,4},{6,5},{7,6},{9,8},{10,9},{11,10},{13,12},{... | collective-permute-start | bytes 3104 | tf_op jit(solution)/shard_map/ppermute | solution.py:30
  236.8 33.1 %collective-permute-start.24 = (f32[1,4096]{1,0:T(1,128)}, f32[1,4096]{1,0:T(1,128)S(1)}, u32[]{:S(2)}, u32[]{:S(2)}) collective-permute-start(f32[1,4096]{1,0:T(1,128)} %get-tuple-element.45), channel_id=1, source_target_pairs={{0,4},{4,8},{8,12},{12,16},{16,20},{20,24},{24,28},{1,5},{5,9},{9,... | collective-permute-start | bytes 49160 | tf_op jit(solution)/shard_map/ppermute | solution.py:27
  242.2 27.8 %collective-permute-start.25 = (f32[1,4096]{1,0:T(1,128)}, f32[1,4096]{1,0:T(1,128)S(1)}, u32[]{:S(2)}, u32[]{:S(2)}) collective-permute-start(f32[1,4096]{1,0:T(1,128)} %get-tuple-element.44), channel_id=1, source_target_pairs={{4,0},{8,4},{12,8},{16,12},{20,16},{24,20},{28,24},{5,1},{9,5},{13... | collective-permute-start | bytes 49160 | tf_op jit(solution)/shard_map/ppermute | solution.py:30
  277.4 34.6 %collective-permute-start.10 = (f32[258,1]{1,0:T(8,128)S(1)}, f32[258,1]{1,0:T(8,128)S(1)}, u32[]{:S(2)}, u32[]{:S(2)}) collective-permute-start(f32[258,1]{1,0:T(8,128)S(1)} %get-tuple-element.37), channel_id=1, source_target_pairs={{0,1},{1,2},{2,3},{4,5},{5,6},{6,7},{8,9},{9,10},{10,11},{12,13},{... | collective-permute-start | bytes 3104 | tf_op jit(solution)/shard_map/ppermute | solution.py:27
  281.4 30.6 %collective-permute-start.11 = (f32[258,1]{1,0:T(8,128)S(1)}, f32[258,1]{1,0:T(8,128)}, u32[]{:S(2)}, u32[]{:S(2)}) collective-permute-start(f32[258,1]{1,0:T(8,128)S(1)} %get-tuple-element.36), channel_id=1, source_target_pairs={{1,0},{2,1},{3,2},{5,4},{6,5},{7,6},{9,8},{10,9},{11,10},{13,12},{... | collective-permute-start | bytes 3104 | tf_op jit(solution)/shard_map/ppermute | solution.py:30
  304.8 33.4 %collective-permute-start.28 = (f32[1,4096]{1,0:T(1,128)}, f32[1,4096]{1,0:T(1,128)S(1)}, u32[]{:S(2)}, u32[]{:S(2)}) collective-permute-start(f32[1,4096]{1,0:T(1,128)} %get-tuple-element.42), channel_id=1, source_target_pairs={{0,4},{4,8},{8,12},{12,16},{16,20},{20,24},{24,28},{1,5},{5,9},{9,... | collective-permute-start | bytes 49160 | tf_op jit(solution)/shard_map/ppermute | solution.py:27
  310.1 28.0 %collective-permute-start.29 = (f32[1,4096]{1,0:T(1,128)}, f32[1,4096]{1,0:T(1,128)S(1)}, u32[]{:S(2)}, u32[]{:S(2)}) collective-permute-start(f32[1,4096]{1,0:T(1,128)} %get-tuple-element.43), channel_id=1, source_target_pairs={{4,0},{8,4},{12,8},{16,12},{20,16},{24,20},{28,24},{5,1},{9,5},{13... | collective-permute-start | bytes 49160 | tf_op jit(solution)/shard_map/ppermute | solution.py:30
  346.3 27.0 %collective-permute-start.14 = (f32[258,1]{1,0:T(8,128)}, f32[258,1]{1,0:T(8,128)S(1)}, u32[]{:S(2)}, u32[]{:S(2)}) collective-permute-start(f32[258,1]{1,0:T(8,128)} %get-tuple-element.34), channel_id=1, source_target_pairs={{0,1},{1,2},{2,3},{4,5},{5,6},{6,7},{8,9},{9,10},{10,11},{12,13},{... | collective-permute-start | bytes 3104 | tf_op jit(solution)/shard_map/ppermute | solution.py:27
  349.7 23.6 %collective-permute-start.15 = (f32[258,1]{1,0:T(8,128)}, f32[258,1]{1,0:T(8,128)S(1)}, u32[]{:S(2)}, u32[]{:S(2)}) collective-permute-start(f32[258,1]{1,0:T(8,128)} %get-tuple-element.35), channel_id=1, source_target_pairs={{1,0},{2,1},{3,2},{5,4},{6,5},{7,6},{9,8},{10,9},{11,10},{13,12},{... | collective-permute-start | bytes 3104 | tf_op jit(solution)/shard_map/ppermute | solution.py:30
  397.5 88.6 %collective-permute-start.32 = (f32[2,64,4096]{2,1,0:T(8,128)S(1)}, f32[2,64,4096]{2,1,0:T(8,128)S(1)}, u32[]{:S(2)}, u32[]{:S(2)}) collective-permute-start(f32[2,64,4096]{2,1,0:T(8,128)S(1)} %get-tuple-element.17), channel_id=1, source_target_pairs={{0,1},{1,0},{2,3},{3,2},{4,5},{5,4},{6,7},{7,6},{8,9},{9,8},{10,11... | collective-permute-start | bytes 6291464 | tf_op jit(solution)/shard_map/ppermute | solution.py:93
  398.1 135.8 %collective-permute-start.33 = (f32[2,64,4096]{2,1,0:T(8,128)S(1)}, f32[2,64,4096]{2,1,0:T(8,128)S(1)}, u32[]{:S(2)}, u32[]{:S(2)}) collective-permute-start(f32[2,64,4096]{2,1,0:T(8,128)S(1)} %get-tuple-element.18), channel_id=1, source_target_pairs={{0,2},{1,3},{2,0},{3,1},{4,6},{5,7},{6,4},{7,5},{8,10},{9,11},{10,... | collective-permute-start | bytes 6291464 | tf_op jit(solution)/shard_map/ppermute | solution.py:93
  398.7 181.8 %collective-permute-start.34 = (f32[2,64,4096]{2,1,0:T(8,128)S(1)}, f32[2,64,4096]{2,1,0:T(8,128)}, u32[]{:S(2)}, u32[]{:S(2)}) collective-permute-start(f32[2,64,4096]{2,1,0:T(8,128)S(1)} %get-tuple-element.19), channel_id=1, source_target_pairs={{0,3},{1,2},{2,1},{3,0},{4,7},{5,6},{6,5},{7,4},{8,11},{9,10},{10,... | collective-permute-start | bytes 6291464 | tf_op jit(solution)/shard_map/ppermute | solution.py:93
  (40 other events, 606.8 us)
